TPU v7x, 32 devices: a whole 2x2x4 slice. The times are simulated.
32 devices in a mesh: trow: 4 (over y, core), tcol: 8 (over z, x).
Axes of the slice: x: 2, y: 2, z: 4, core: 2. Of those that a mesh axis runs over, the one named last changes fastest.
Arguments:
- response: bfloat16 [4096, 16384], P('trow', 'tcol'), may hold values from -0.046875 to 0.046875
- test_matrix: bfloat16 [1024, 192], P(('trow', 'tcol')), may hold values from -6 to 6
- slopes: bfloat16 [16384, 256], P('tcol', 'trow'), may hold values from -6 to 6
- ranks: int32 [4, 16], P('trow', 'tcol'), may hold values from 16 to 192, as said below
Outputs:
- commands: float32 [4096, 256], P(('trow', 'tcol'))
Inputs may be any that keep to these rules, and one draw needn't show every extreme that they name: ranks of tiles near the diagonal tend to be higher, and every tile's sketch has full column rank and is well conditioned.
All inputs are finite; a program needn't handle non-finite values.
Results may differ from a plain program's by a relative error of at most 0.014.
Values may be sent and summed in bfloat16 or wider, within the bound.
A program may use at most 64 MiB of HBM per device.

v0:
```python
import jax
import jax.numpy as jnp
from jax import lax
from jax.sharding import PartitionSpec as P


def fetch_frames(slopes):
    return lax.all_gather(slopes, "trow", axis=1, tiled=True)


def on_device(response, test_matrix, slopes, ranks):
    highest = lax.Precision.HIGHEST
    tile_rows = ranks.shape[0]
    tile_cols = ranks.shape[1]
    width = response.shape[0] // tile_rows
    sketch_width = test_matrix.shape[1]
    tiles = response.reshape(tile_rows, width, tile_cols, width)
    row_block = lax.all_gather(test_matrix, "tcol", axis=0, tiled=True)
    sketch = jnp.einsum(
        "rick,kj->rcij",
        tiles,
        lax.all_gather(row_block, "trow", axis=0, tiled=True),
        preferred_element_type=jnp.float32,
    )
    gram = jnp.einsum("rcik,rcil->rckl", sketch, sketch, precision=highest)
    chol = jnp.linalg.cholesky(gram)
    basis = jax.scipy.linalg.solve_triangular(chol, jnp.swapaxes(sketch, 2, 3), lower=True)
    slots = jnp.arange(sketch_width, dtype=jnp.int32)
    keep = (slots[None, None, :] < ranks[:, :, None]).astype(jnp.float32)
    basis = (basis * keep[:, :, :, None]).astype(jnp.bfloat16)
    factor = jnp.einsum("rcsi,ricj->rcsj", basis, tiles, preferred_element_type=jnp.float32).astype(
        jnp.bfloat16
    )
    frames = fetch_frames(slopes)
    frame_count = frames.shape[1]
    frame_tiles = frames.reshape(tile_cols, width, frame_count)
    coeff = jnp.einsum(
        "rcsj,cjf->rcsf", factor, frame_tiles, preferred_element_type=jnp.float32
    ).astype(jnp.bfloat16)
    share_rows = tile_rows * width // lax.axis_size("tcol")
    summed = jnp.einsum("rcsi,rcsf->rif", basis, coeff, preferred_element_type=jnp.float32)
    summed_all = lax.psum(
        summed.reshape(tile_rows * width, frame_count).astype(jnp.bfloat16), "tcol"
    ).astype(jnp.float32)
    result = lax.dynamic_slice_in_dim(
        summed_all, lax.axis_index("tcol") * share_rows, share_rows, 0
    )
    return result


def solution(mesh):
    return jax.shard_map(
        on_device,
        mesh=mesh,
        in_specs=(
            P("trow", "tcol"),
            P(("trow", "tcol"), None),
            P("tcol", "trow"),
            P("trow", "tcol"),
        ),
        out_specs=P(("trow", "tcol"), None),
        check_vma=False,
    )
```

profile of v0, /device:TPU:0, one launch (start us, length us, event | category | flops | bytes accessed | tf_op | source)
XLA Modules:
  0.0 238.7 jit_solution(7302587469162838817)
XLA Ops:
  6.5 0.0 all-gather.2.cloned.1.call-start
  6.5 0.7 all-gather.2.cloned.1.call-update
  7.3 0.0 all-reduce.5.cloned.1.call-start
  7.4 32.5 %all_gather.9 = bf16[256,192]{1,0:T(8,128)(2,1)S(1)} all-gather(bf16[32,192]{1,0:T(8,128)(2,1)} %param.5), channel_id=1, replica_groups=mesh['trow'=4,'tcol'=8] {'tcol'}, dimensions={0}, use_global_device_ids=true | all-gather | bytes 110592 | tf_op jit(solution)/shard_map/all_gather | solution.py:18
  39.9 0.1 copy.21
  40.1 6.5 %all_gather.10 = bf16[1024,192]{0,1:T(8,128)(2,1)S(1)} all-gather(bf16[256,192]{0,1:T(8,128)(2,1)S(1)} %copy.21), channel_id=1, replica_groups=mesh['trow'=4,'tcol'=8] {'trow'}, dimensions={0}, use_global_device_ids=true | all-gather | bytes 491520 | tf_op jit(solution)/shard_map/all_gather | solution.py:22
  46.5 3.7 %fusion.2 = f32[192,1024,2]{1,0,2:T(8,128)S(1)} fusion(bf16[128,2,8,1024]{3,2,1,0:T(8,128)(2,1)} %bitcast.77, bf16[1024,192]{0,1:T(8,128)(2,1)S(1)} %all_gather.10), kind=kOutput, calls=%fused_computation.2 | convolution fusion | flops 805306368 | bytes 6160384 | tf_op jit(solution)/shard_map/rick,kj->rcij/dot_general | solution.py:19
  50.3 1.7 fusion.7
  51.9 0.2 copy.24
  52.1 0.1 fusion.16
  52.2 23.6 %custom-call.17 = f32[1,2,128,128]{3,2,1,0:T(8,128)S(1)} custom-call(f32[1,2,128,128]{3,2,1,0:T(8,128)S(1)} %cholesky.132), custom_call_target="Cholesky" | custom-call | tf_op jit(solution)/shard_map/jit(cholesky)/cholesky | solution.py:26
  75.9 19.7 %custom-call.18 = f32[1,2,1,128,128]{3,4,2,1,0:T(8,128)S(1)} custom-call(f32[1,2,1,128,128]{4,3,2,1,0:T(8,128)S(1)} %get-tuple-element.26), custom_call_target="InvertDiagBlocksLowerTriangular" | custom-call | tf_op jit(solution)/shard_map/jit(cholesky)/cholesky | solution.py:26
  95.6 0.0 copy-start
  95.6 0.2 bitcast_dynamic-update-slice_fusion
  95.9 0.2 fusion.13
  96.1 11.7 %custom-call.19 = f32[1,2,64,64]{3,2,1,0:T(8,128)S(1)} custom-call(f32[1,2,64,64]{3,2,1,0:T(8,128)S(1)} %fusion.13), custom_call_target="Cholesky" | custom-call | tf_op jit(solution)/shard_map/jit(cholesky)/cholesky | solution.py:26
  107.9 0.1 compare_reduce_fusion
  108.0 0.1 compare_reduce_fusion.1
  108.1 0.1 bitcast_select_fusion
  108.3 0.1 fusion.18
  108.5 39.5 %custom-call.20 = f32[2,2,128,128]{2,3,1,0:T(8,128)S(1)} custom-call(f32[2,2,128,128]{3,2,1,0:T(8,128)S(1)} %pad_maximum_fusion), custom_call_target="InvertDiagBlocksLowerTriangular" | custom-call | tf_op jit(solution)/shard_map/jit(_solve_triangular)/vmap()/triangular_solve | solution.py:27
  148.0 0.0 copy-done
  148.0 0.1 compare_convert_fusion
  148.1 1.1 fusion.14
  149.2 0.7 convolution_subtract_fusion
  149.9 0.6 fusion.22
  150.5 2.0 fusion.9
  152.5 1.5 copy.30
  154.0 2.8 %fusion.12 = bf16[1024,256]{1,0:T(8,128)(2,1)} fusion(bf16[2,192,1024]{2,1,0:T(8,128)(2,1)} %fusion.9, bf16[2,1024,256]{2,1,0:T(8,128)(2,1)S(1)} %bitcast.75, f32[2,64,1024]{2,1,0:T(8,128)S(1)} %fusion.22, f32[2,128,1024]{2,1,0:T(8,128)S(1)} %fusion.14, f32[2,192]{1,0:T(2,128)S(1)} %compare_convert_fusion), kind=kOutput, calls=%fused_computation.12 | convolution fusion | flops 404193280 | bytes 3933696 | tf_op jit(solution)/shard_map/rcsi,rcsf->rif/dot_general | solution.py:41
  156.8 0.0 all-reduce.5.cloned.1.call-update
  156.8 73.5 %all-reduce.5.cloned.1.call-done = bf16[1024,256]{1,0:T(8,128)(2,1)} async-done(((bf16[1024,256]{1,0:T(8,128)(2,1)}), bf16[1024,256]{1,0:T(8,128)(2,1)}) %all-reduce.5.cloned.1.call-update) | async-done | bytes 524304 | tf_op jit(solution)/shard_map/psum | solution.py:42
  230.3 1.5 dynamic-slice_convert_fusion
  (17 shorter events, 0.2 us)
Async XLA Ops:
  6.5 146.0 %all-gather.2.cloned.1.call-start = ((), (), s32[]{:S(2)}) async-start(), calls=%async_computation | async-start | bytes 1310720 | tf_op jit(solution)/shard_map/all_gather | solution.py:8
  7.3 223.1 %all-reduce.5.cloned.1.call-start = ((), (), s32[]{:S(2)}) async-start(), calls=%async_computation.1 | async-start | bytes 1048576 | tf_op jit(solution)/shard_map/psum | solution.py:42
  95.6 52.4 %copy-start = (s32[1,2]{1,0:T(1,128)S(1)}, s32[1,2]{1,0:T(1,128)}, u32[]{:S(2)}) copy-start(s32[1,2]{1,0:T(1,128)} %param.7) | copy-start | bytes 28
  148.1 2.4 %copy-start.1 = (bf16[1024,2048]{1,0:T(8,128)(2,1)S(1)}, bf16[1024,2048]{1,0:T(8,128)(2,1)}, u32[]{:S(2)}) copy-start(bf16[1024,2048]{1,0:T(8,128)(2,1)} %param.4) | copy-start | bytes 12582916
Sparse Core Ops, SparseCore 0:
  8.9 19.4 all-gather.1
  156.9 73.3 all-reduce.4
where the time goes:
time: 239 us
  other arithmetic  96.8 us (41%)
  waiting for transfers between devices  74.2 us (31%)
  blocking collectives  39 us (16%)
  between operations  13.6 us (6%)
  matrix products  13 us (5%)
    psum x1, waiting for transfers between devices, on_device(): lax.psum(summed.reshape(tile_rows * width, frame_count).astype(jnp.bfloat...  73.5 us
    another operation x10, other arithmetic, on_device(): chol = jnp.linalg.cholesky(gram)  55.4 us
    another operation x7, other arithmetic, on_device(): jax.scipy.linalg.solve_triangular(chol, jnp.swapaxes(sketch, 2, 3), lower...  39.8 us
    all_gather x1, blocking collectives, on_device(): row_block = lax.all_gather(test_matrix, 'tcol', axis=0, tiled=True)  32.5 us
    all_gather x1, blocking collectives, on_device(): lax.all_gather(row_block, 'trow', axis=0, tiled=True)  6.49 us
  transfers between devices with their start and end apart: 2, of which 1 were waited for; matrix products, arithmetic and copies ran while one was open for 44% of the time, Pallas kernels for 0%

commit v1 on v0

--- a/solution.py
+++ b/solution.py
@@ -15,7 +15,12 @@
     width = response.shape[0] // tile_rows
     sketch_width = test_matrix.shape[1]
     tiles = response.reshape(tile_rows, width, tile_cols, width)
-    row_block = lax.all_gather(test_matrix, "tcol", axis=0, tiled=True)
+    ring = [test_matrix]
+    for hop in range(7):
+        ring.append(lax.ppermute(ring[-1], "tcol", [(dev, (dev + 1) % 8) for dev in range(8)]))
+    row_block = jnp.roll(
+        jnp.concatenate(ring[::-1], axis=0), (lax.axis_index("tcol") + 1) * ring[0].shape[0], axis=0
+    )
     sketch = jnp.einsum(
         "rick,kj->rcij",
         tiles,

time: 239 us -> 250 us (1.046)
  waiting for transfers between devices: 74.2 us -> 115 us
  blocking collectives: 39 us -> 6.86 us
  starting transfers between devices: 0.04 us -> 3.07 us
    ppermute x0 -> x7, waiting for transfers between devices: none -> 45.2 us  [on_device(): lax.ppermute(ring[-1], 'tcol', [(dev, (dev + 1) % 8) for dev in range(8)])]
    all_gather x1 -> x0, blocking collectives: 32.5 us -> none  [on_device(): row_block = lax.all_gather(test_matrix, 'tcol', axis=0, tiled=True)]
    psum x1, waiting for transfers between devices: 73.5 us -> 69.9 us  [on_device(): lax.psum(summed.reshape(tile_rows * width, frame_count).astype(jnp.bfloat...]
    ppermute x0 -> x7, starting transfers between devices: none -> 3.03 us  [on_device(): lax.ppermute(ring[-1], 'tcol', [(dev, (dev + 1) % 8) for dev in range(8)])]
  transfers between devices with their start and end apart: 2 -> 9, of which waited for: 1 -> 8; matrix products, arithmetic and copies ran while one was open for 44% -> 42% of each run, Pallas kernels for 0% -> 0%
where the time goes in v1:
time: 250 us
  waiting for transfers between devices  115 us (46%)
  other arithmetic  97.5 us (39%)
  between operations  13.7 us (5%)
  matrix products  10.9 us (4%)
  blocking collectives  6.86 us (3%)
  starting transfers between devices  3.07 us (1%)
  local copies, waits for them, and re-layouts  2.95 us (1%)
    psum x1, waiting for transfers between devices, on_device(): lax.psum(summed.reshape(tile_rows * width, frame_count).astype(jnp.bfloat...  69.9 us
    another operation x10, other arithmetic, on_device(): chol = jnp.linalg.cholesky(gram)  55.4 us
    ppermute x7, waiting for transfers between devices, on_device(): lax.ppermute(ring[-1], 'tcol', [(dev, (dev + 1) % 8) for dev in range(8)])  45.2 us
    another operation x7, other arithmetic, on_device(): jax.scipy.linalg.solve_triangular(chol, jnp.swapaxes(sketch, 2, 3), lower...  39.8 us
    all_gather x1, blocking collectives, on_device(): lax.all_gather(row_block, 'trow', axis=0, tiled=True)  6.86 us
  transfers between devices with their start and end apart: 9, of which 8 were waited for; matrix products, arithmetic and copies ran while one was open for 42% of the time, Pallas kernels for 0%

profile of v1, /device:TPU:0, one launch (start us, length us, event | category | flops | bytes accessed | tf_op | source)
XLA Modules:
  0.0 250.1 jit_solution(12288929542192047939)
XLA Ops:
  6.5 0.8 copy.15
  7.4 3.0 %collective-permute-start = (bf16[32,192]{0,1:T(8,128)(2,1)S(1)}, bf16[32,192]{0,1:T(8,128)(2,1)S(1)}, u32[]{:S(2)}, u32[]{:S(2)}) collective-permute-start(bf16[32,192]{0,1:T(8,128)(2,1)S(1)} %copy.15), channel_id=1, source_target_pairs={{0,1},{1,2},{2,3},{3,4},{4,5},{5,6},{6,7},{7,0},{8,9},{9,10},{10,1... | collective-permute-start | bytes 36872 | tf_op jit(solution)/shard_map/ppermute | solution.py:20
  10.5 5.0 %collective-permute-done = bf16[32,192]{0,1:T(8,128)(2,1)S(1)} collective-permute-done((bf16[32,192]{0,1:T(8,128)(2,1)S(1)}, bf16[32,192]{0,1:T(8,128)(2,1)S(1)}, u32[]{:S(2)}, u32[]{:S(2)}) %collective-permute-start) | collective-permute-done | bytes 12320 | tf_op jit(solution)/shard_map/ppermute | solution.py:20
  15.5 0.7 compare_convert_fusion
  16.2 6.1 %collective-permute-done.1 = bf16[32,192]{0,1:T(8,128)(2,1)S(1)} collective-permute-done((bf16[32,192]{0,1:T(8,128)(2,1)S(1)}, bf16[32,192]{0,1:T(8,128)(2,1)S(1)}, u32[]{:S(2)}, u32[]{:S(2)}) %collective-permute-start.1) | collective-permute-done | bytes 12320 | tf_op jit(solution)/shard_map/ppermute | solution.py:20
  22.3 6.8 %collective-permute-done.2 = bf16[32,192]{0,1:T(8,128)(2,1)S(1)} collective-permute-done((bf16[32,192]{0,1:T(8,128)(2,1)S(1)}, bf16[32,192]{0,1:T(8,128)(2,1)S(1)}, u32[]{:S(2)}, u32[]{:S(2)}) %collective-permute-start.2) | collective-permute-done | bytes 12320 | tf_op jit(solution)/shard_map/ppermute | solution.py:20
  29.1 6.8 %collective-permute-done.3 = bf16[32,192]{0,1:T(8,128)(2,1)S(1)} collective-permute-done((bf16[32,192]{0,1:T(8,128)(2,1)S(1)}, bf16[32,192]{0,1:T(8,128)(2,1)S(1)}, u32[]{:S(2)}, u32[]{:S(2)}) %collective-permute-start.3) | collective-permute-done | bytes 12320 | tf_op jit(solution)/shard_map/ppermute | solution.py:20
  35.9 7.1 %collective-permute-done.4 = bf16[32,192]{0,1:T(8,128)(2,1)S(1)} collective-permute-done((bf16[32,192]{0,1:T(8,128)(2,1)S(1)}, bf16[32,192]{0,1:T(8,128)(2,1)S(1)}, u32[]{:S(2)}, u32[]{:S(2)}) %collective-permute-start.4) | collective-permute-done | bytes 12320 | tf_op jit(solution)/shard_map/ppermute | solution.py:20
  43.0 6.8 %collective-permute-done.5 = bf16[32,192]{0,1:T(8,128)(2,1)S(1)} collective-permute-done((bf16[32,192]{0,1:T(8,128)(2,1)S(1)}, bf16[32,192]{0,1:T(8,128)(2,1)S(1)}, u32[]{:S(2)}, u32[]{:S(2)}) %collective-permute-start.5) | collective-permute-done | bytes 12320 | tf_op jit(solution)/shard_map/ppermute | solution.py:20
  49.8 6.8 %collective-permute-done.6 = bf16[32,192]{0,1:T(8,128)(2,1)S(1)} collective-permute-done((bf16[32,192]{0,1:T(8,128)(2,1)S(1)}, bf16[32,192]{0,1:T(8,128)(2,1)S(1)}, u32[]{:S(2)}, u32[]{:S(2)}) %collective-permute-start.6) | collective-permute-done | bytes 12320 | tf_op jit(solution)/shard_map/ppermute | solution.py:20
  56.6 0.3 concatenate.18
  57.0 6.9 %all_gather.6 = bf16[1024,192]{0,1:T(8,128)(2,1)S(1)} all-gather(bf16[256,192]{0,1:T(8,128)(2,1)S(1)} %constant_dynamic-slice_fusion), channel_id=1, replica_groups=mesh['trow'=4,'tcol'=8] {'trow'}, dimensions={0}, use_global_device_ids=true | all-gather | bytes 491520 | tf_op jit(solution)/shard_map/all_gather | solution.py:27
  63.8 3.7 %fusion.2 = f32[192,1024,2]{1,0,2:T(8,128)S(1)} fusion(bf16[128,2,8,1024]{3,2,1,0:T(8,128)(2,1)} %bitcast.77, bf16[1024,192]{0,1:T(8,128)(2,1)S(1)} %all_gather.6), kind=kOutput, calls=%fused_computation.2 | convolution fusion | flops 805306368 | bytes 6160384 | tf_op jit(solution)/shard_map/rick,kj->rcij/dot_general | solution.py:24
  67.5 1.7 fusion.7
  69.2 0.2 copy.20
  69.5 23.6 %custom-call.17 = f32[1,2,128,128]{3,2,1,0:T(8,128)S(1)} custom-call(f32[1,2,128,128]{3,2,1,0:T(8,128)S(1)} %cholesky.132), custom_call_target="Cholesky" | custom-call | tf_op jit(solution)/shard_map/jit(cholesky)/cholesky | solution.py:31
  93.2 19.7 %custom-call.18 = f32[1,2,1,128,128]{3,4,2,1,0:T(8,128)S(1)} custom-call(f32[1,2,1,128,128]{4,3,2,1,0:T(8,128)S(1)} %get-tuple-element.26), custom_call_target="InvertDiagBlocksLowerTriangular" | custom-call | tf_op jit(solution)/shard_map/jit(cholesky)/cholesky | solution.py:31
  112.9 0.2 bitcast_dynamic-update-slice_fusion
  113.1 0.2 fusion.13
  113.3 11.7 %custom-call.19 = f32[1,2,64,64]{3,2,1,0:T(8,128)S(1)} custom-call(f32[1,2,64,64]{3,2,1,0:T(8,128)S(1)} %fusion.13), custom_call_target="Cholesky" | custom-call | tf_op jit(solution)/shard_map/jit(cholesky)/cholesky | solution.py:31
  125.1 0.1 compare_reduce_fusion
  125.2 0.1 compare_reduce_fusion.1
  125.4 0.1 bitcast_select_fusion
  125.7 39.5 %custom-call.20 = f32[2,2,128,128]{2,3,1,0:T(8,128)S(1)} custom-call(f32[2,2,128,128]{3,2,1,0:T(8,128)S(1)} %pad_maximum_fusion), custom_call_target="InvertDiagBlocksLowerTriangular" | custom-call | tf_op jit(solution)/shard_map/jit(_solve_triangular)/vmap()/triangular_solve | solution.py:32
  165.2 1.1 fusion.14
  166.3 0.7 convolution_subtract_fusion
  167.0 0.6 fusion.22
  167.7 1.0 fusion.9
  168.7 1.5 copy.30
  170.2 1.6 fusion.12
  171.8 69.9 %all-reduce.5.cloned.1.call-done = bf16[1024,256]{1,0:T(8,128)(2,1)} async-done(((bf16[1024,256]{1,0:T(8,128)(2,1)}), bf16[1024,256]{1,0:T(8,128)(2,1)}) %all-reduce.5.cloned.1.call-update) | async-done | bytes 524304 | tf_op jit(solution)/shard_map/psum | solution.py:47
  241.7 1.5 dynamic-slice_convert_fusion
  (30 shorter events, 0.6 us)
Async XLA Ops:
  6.5 162.2 %all-gather.2.cloned.1.call-start = ((), (), s32[]{:S(2)}) async-start(), calls=%async_computation | async-start | bytes 1310720 | tf_op jit(solution)/shard_map/all_gather | solution.py:8
  7.4 8.1 %collective-permute-start = (bf16[32,192]{0,1:T(8,128)(2,1)S(1)}, bf16[32,192]{0,1:T(8,128)(2,1)S(1)}, u32[]{:S(2)}, u32[]{:S(2)}) collective-permute-start(bf16[32,192]{0,1:T(8,128)(2,1)S(1)} %copy.15), channel_id=1, source_target_pairs={{0,1},{1,2},{2,3},{3,4},{4,5},{5,6},{6,7},{7,0},{8,9},{9,10},{10,1... | collective-permute-start | bytes 36872 | tf_op jit(solution)/shard_map/ppermute | solution.py:20
  10.4 231.3 %all-reduce.5.cloned.1.call-start = ((), (), s32[]{:S(2)}) async-start(), calls=%async_computation.1 | async-start | bytes 1048576 | tf_op jit(solution)/shard_map/psum | solution.py:47
  15.5 6.8 %collective-permute-start.1 = (bf16[32,192]{0,1:T(8,128)(2,1)S(1)}, bf16[32,192]{0,1:T(8,128)(2,1)S(1)}, u32[]{:S(2)}, u32[]{:S(2)}) collective-permute-start(bf16[32,192]{0,1:T(8,128)(2,1)S(1)} %collective-permute-done), channel_id=1, source_target_pairs={{0,1},{1,2},{2,3},{3,4},{4,5},{5,6},{6,7},{7,0},{8,9},{9,10},{10,1... | collective-permute-start | bytes 36872 | tf_op jit(solution)/shard_map/ppermute | solution.py:20
  22.3 6.8 %collective-permute-start.2 = (bf16[32,192]{0,1:T(8,128)(2,1)S(1)}, bf16[32,192]{0,1:T(8,128)(2,1)S(1)}, u32[]{:S(2)}, u32[]{:S(2)}) collective-permute-start(bf16[32,192]{0,1:T(8,128)(2,1)S(1)} %collective-permute-done.1), channel_id=1, source_target_pairs={{0,1},{1,2},{2,3},{3,4},{4,5},{5,6},{6,7},{7,0},{8,9},{9,10},{10,1... | collective-permute-start | bytes 36872 | tf_op jit(solution)/shard_map/ppermute | solution.py:20
  29.1 6.8 %collective-permute-start.3 = (bf16[32,192]{0,1:T(8,128)(2,1)S(1)}, bf16[32,192]{0,1:T(8,128)(2,1)S(1)}, u32[]{:S(2)}, u32[]{:S(2)}) collective-permute-start(bf16[32,192]{0,1:T(8,128)(2,1)S(1)} %collective-permute-done.2), channel_id=1, source_target_pairs={{0,1},{1,2},{2,3},{3,4},{4,5},{5,6},{6,7},{7,0},{8,9},{9,10},{10,1... | collective-permute-start | bytes 36872 | tf_op jit(solution)/shard_map/ppermute | solution.py:20
  35.9 7.1 %collective-permute-start.4 = (bf16[32,192]{0,1:T(8,128)(2,1)S(1)}, bf16[32,192]{0,1:T(8,128)(2,1)S(1)}, u32[]{:S(2)}, u32[]{:S(2)}) collective-permute-start(bf16[32,192]{0,1:T(8,128)(2,1)S(1)} %collective-permute-done.3), channel_id=1, source_target_pairs={{0,1},{1,2},{2,3},{3,4},{4,5},{5,6},{6,7},{7,0},{8,9},{9,10},{10,1... | collective-permute-start | bytes 36872 | tf_op jit(solution)/shard_map/ppermute | solution.py:20
  43.0 6.8 %collective-permute-start.5 = (bf16[32,192]{0,1:T(8,128)(2,1)S(1)}, bf16[32,192]{0,1:T(8,128)(2,1)S(1)}, u32[]{:S(2)}, u32[]{:S(2)}) collective-permute-start(bf16[32,192]{0,1:T(8,128)(2,1)S(1)} %collective-permute-done.4), channel_id=1, source_target_pairs={{0,1},{1,2},{2,3},{3,4},{4,5},{5,6},{6,7},{7,0},{8,9},{9,10},{10,1... | collective-permute-start | bytes 36872 | tf_op jit(solution)/shard_map/ppermute | solution.py:20
  49.8 6.8 %collective-permute-start.6 = (bf16[32,192]{0,1:T(8,128)(2,1)S(1)}, bf16[32,192]{0,1:T(8,128)(2,1)S(1)}, u32[]{:S(2)}, u32[]{:S(2)}) collective-permute-start(bf16[32,192]{0,1:T(8,128)(2,1)S(1)} %collective-permute-done.5), channel_id=1, source_target_pairs={{0,1},{1,2},{2,3},{3,4},{4,5},{5,6},{6,7},{7,0},{8,9},{9,10},{10,1... | collective-permute-start | bytes 36872 | tf_op jit(solution)/shard_map/ppermute | solution.py:20
  165.2 2.4 copy-start
Sparse Core Ops, SparseCore 0:
  10.5 17.7 all-gather.1
  172.0 69.7 all-reduce.4
